TPU v7x, 512 devices: a whole 4x8x8 slice. The times are simulated.
512 devices in a mesh: depth: 8 (over x, core), sx: 8 (over z), sy: 8 (over y).
Axes of the slice: x: 4, y: 8, z: 8, core: 2. Of those that a mesh axis runs over, the one named last changes fastest.
Arguments:
- transmission: bfloat16 [16, 2, 2048, 2048], P('depth', None, 'sx', 'sy')
- incident: bfloat16 [16, 128, 2, 256, 256], P('depth', ('sx', 'sy')), may hold values from -6 to 6
- exit_adjoint: bfloat16 [128, 2, 256, 256], P(('sx', 'sy')), may hold values from -6 to 6
- propagator_phase: float32 [256, 256], replicated, may hold values from -3.140625 to 3.140625
- scan_anchor: int32 [128, 2], P(('sx', 'sy')), may hold values from -128 to 1919, as said below
- live_count: int32 [64], P(('sx', 'sy')), may hold values from 1 to 2, as said below
Outputs:
- gradient: float32 [16, 2, 2048, 2048], P('depth', None, 'sx', 'sy')
Inputs may be any that keep to these rules, and one draw needn't show every extreme that they name: `scan_anchor`: the slot at position p of the device at indices (a, b) of (sx, sy), slot a * 2 * 8 + b * 2 + p, has its x anchor in [a * 256 - 256 // 2, a * 256 + 256 - 256 // 2) and its y anchor in [b * 256 - 256 // 2, b * 256 + 256 - 256 // 2). Both ends of the whole range are taken in every draw. The live slots of a device are its first live_count slots; some device has all 2 slots live and some device exactly one.
All inputs are finite; a program needn't handle non-finite values.
Results may differ from a plain program's by a relative error of at most 0.0003.
Values may be sent and summed in bfloat16 or wider, within the bound.
A program may use at most 128 MiB of HBM per device.

v0:
```python
import functools

import ml_dtypes
import numpy as np
import jax
import jax.numpy as jnp
from jax import lax
from jax.experimental import pallas as pl
from jax.experimental.pallas import tpu as pltpu
from jax.sharding import PartitionSpec as P

TILE = 256
HALF = 128
MESH = pl.DeviceIdType.MESH
F32 = jnp.float32
BF16 = jnp.bfloat16


def dft_tables():
    n = np.arange(HALF)
    angle = 2.0 * np.pi * ((n[:, None] * n[None, :]) % HALF) / HALF
    c, s = np.cos(angle) / 16.0, np.sin(angle) / 16.0
    m = np.block([[c, s], [-s, c]])
    out = []
    for a in (m, m.T):
        head = a.astype(ml_dtypes.bfloat16)
        out += [head, (a - head.astype(np.float64)).astype(ml_dtypes.bfloat16)]
    return np.stack(out)


def twiddles():
    n = 2.0 * np.pi * np.arange(HALF) / TILE
    rows = np.stack([np.cos(n), np.sin(n)])
    return (
        np.broadcast_to(rows[:, :, None], (2, HALF, HALF)).astype(np.float32),
        np.broadcast_to(rows[:, None, :], (2, 8, HALF)).astype(np.float32),
    )


def halves(x):
    head = x.astype(BF16)
    return head, (x - head.astype(F32)).astype(BF16)


def conj_times(ar, ai, br, bi):
    return ar * br + ai * bi, ar * bi - ai * br


def dot(a, b):
    return jnp.dot(a, b, preferred_element_type=F32)


def kernel(
    sizes,
    t_hbm,
    inc_hbm,
    exit_hbm,
    phase_hbm,
    m_hbm,
    rows_hbm,
    lane_ref,
    anchor_ref,
    live_ref,
    out_hbm,
    t_own,
    t_alt,
    t_eff,
    inc,
    exit_v,
    phase,
    rot,
    m_v,
    rows_v,
    waves,
    middle,
    sent,
    zbuf,
    ebuf,
    g_own,
    g_alt,
    g_in,
    load_sem,
    t_send,
    t_recv,
    w_send,
    w_recv,
    g_send,
    g_recv,
    out_sem,
):
    n_depth, n_sx, n_sy = sizes
    d, sx, sy = lax.axis_index("depth"), lax.axis_index("sx"), lax.axis_index("sy")
    last = n_depth - 1

    def at(dx, dy):
        return (d, lax.rem(sx + dx + n_sx, n_sx), lax.rem(sy + dy + n_sy, n_sy))

    around = [(i, j) for i in (-1, 0, 1) for j in (-1, 0, 1) if (i, j) != (0, 0)]

    loads = [
        pltpu.make_async_copy(src, dst, load_sem.at[i])
        for i, (src, dst) in enumerate(
            [
                (phase_hbm, phase),
                (m_hbm, m_v),
                (rows_hbm, rows_v),
                (exit_hbm, exit_v),
                (inc_hbm, inc),
                (t_hbm, t_own),
            ]
        )
    ]
    for c in loads:
        c.start()

    barrier = pltpu.get_barrier_semaphore()
    for i, j in around:
        pl.semaphore_signal(barrier, inc=1, device_id=at(i, j), device_id_type=MESH)

    for step in (1, last):
        near = (lax.rem(d + step, n_depth), sx, sy)
        pl.semaphore_signal(barrier, inc=1, device_id=near, device_id_type=MESH)
    pl.semaphore_wait(barrier, len(around) + 2)

    full = pl.ds(0, TILE)
    part = [pl.ds(0, HALF), pl.ds(HALF, HALF)]
    toward = [-1, 1]
    pieces = (
        [(0, part[p], full, (toward[p], 0)) for p in (0, 1)]
        + [(1, full, part[q], (0, toward[q])) for q in (0, 1)]
        + [(2, part[p], part[q], (toward[p], toward[q])) for p in (0, 1) for q in (0, 1)]
    )

    def t_copies(li):
        return [
            pltpu.make_async_remote_copy(
                src_ref=t_hbm.at[li, :, rows, lanes],
                dst_ref=t_alt.at[li, kind, :, rows, lanes],
                send_sem=t_send.at[li * 8 + i],
                recv_sem=t_recv.at[li * 8 + i],
                device_id=at(*way),
                device_id_type=MESH,
            )
            for i, (kind, rows, lanes, way) in enumerate(pieces)
        ]

    def g_copies(li):
        return [
            pltpu.make_async_remote_copy(
                src_ref=g_alt.at[li, kind, :, rows, lanes],
                dst_ref=g_in.at[li, kind, :, rows, lanes],
                send_sem=g_send.at[li * 8 + i],
                recv_sem=g_recv.at[li * 8 + i],
                device_id=at(-way[0], -way[1]),
                device_id_type=MESH,
            )
            for i, (kind, rows, lanes, way) in enumerate(pieces)
        ]

    def w_copy(slot, h):
        return pltpu.make_async_remote_copy(
            src_ref=sent.at[slot, h],
            dst_ref=waves.at[slot, h],
            send_sem=w_send.at[slot * 2 + h],
            recv_sem=w_recv.at[slot * 2 + h],
            device_id=(lax.rem(d + last, n_depth), sx, sy),
            device_id_type=MESH,
        )

    for li in (1, 0):
        for c in t_copies(li):
            c.start()

    def offsets(slot):
        return anchor_ref[slot, 0] - sx * TILE, anchor_ref[slot, 1] - sy * TILE

    def spans(slot):
        ax, ay = offsets(slot)
        out = []
        for a, k, n in ((ax, sx, n_sx), (ay, sy, n_sy)):
            low, high = jnp.maximum(a, 0), TILE + jnp.minimum(a, 0)
            out.append((low, high, jnp.where(k < n - 1, low, 0), jnp.where(k > 0, high, TILE)))
        return out

    def masks(slot, h):
        (lx, hx, olx, ohx), (ly, hy, oly, ohy) = spans(slot)
        r = lax.broadcasted_iota(jnp.int32, (HALF, TILE), 0) + h * HALF
        c = lax.broadcasted_iota(jnp.int32, (HALF, TILE), 1)
        own_x = (r >= lx) & (r < hx)
        own_y = (c >= ly) & (c < hy)
        alt_x = (r < olx) | (r >= ohx)
        alt_y = (c < oly) | (c >= ohy)
        return own_x, own_y, alt_x, alt_y

    def rolled(slot, fields):
        ax, ay = offsets(slot)
        i = lax.broadcasted_iota(jnp.int32, (TILE, TILE), 0)
        j = lax.broadcasted_iota(jnp.int32, (TILE, TILE), 1)
        by_rows = jnp.where(((j + ax - i) & (TILE - 1)) == 0, 1.0, 0.0).astype(BF16)
        by_lanes = jnp.where(((i + ay - j) & (TILE - 1)) == 0, 1.0, 0.0).astype(BF16)
        return [dot(by_rows, dot(f, by_lanes).astype(BF16)) for f in fields]

    for c in loads[:5]:
        c.wait()

    @pl.when(d == last)
    def _():
        for slot in (0, 1):
            alive = jnp.where(slot < live_ref[0], 1.0, 0.0).astype(F32)
            for k, f in enumerate(rolled(slot, [exit_v[slot, 0], exit_v[slot, 1]])):
                for h in (0, 1):
                    waves[slot, h, k] = f[h * HALF : (h + 1) * HALF] * alive

    i = lax.broadcasted_iota(jnp.int32, (TILE, TILE), 0)
    j = lax.broadcasted_iota(jnp.int32, (TILE, TILE), 1)
    deal = jnp.where(i == jnp.where(j < HALF, 2 * j, 2 * j - (TILE - 1)), 1.0, 0.0).astype(BF16)
    deal_rows = jnp.where(j == jnp.where(i < HALF, 2 * i, 2 * i - (TILE - 1)), 1.0, 0.0).astype(BF16)
    p = phase[...]
    p0 = p.astype(BF16)
    p1, p2 = halves(p - p0.astype(F32))
    f0, f1, f2 = [dot(deal_rows, dot(q, deal).astype(BF16)) for q in (p0, p1, p2)]
    phase[...] = (f0 + f1) + f2
    for h in (0, 1):
        ordered = phase[part[h], :]
        rot[0, h] = jnp.cos(ordered)
        rot[1, h] = jnp.sin(ordered)

    def roll_incident(slot):
        got = rolled(slot, [inc[li, slot, k] for li in (0, 1) for k in (0, 1)])
        for n, f in enumerate(got):
            inc[n // 2, slot, n % 2] = f.astype(BF16)

    for slot in (0, 1):
        roll_incident(slot)

    zero = jnp.zeros((HALF, TILE), F32)

    def window(li, slot):
        for h in (0, 1):
            own_x, own_y, alt_x, alt_y = masks(slot, h)
            rows = part[h]
            for k in (0, 1):
                here = t_own[li, k, rows, :].astype(F32)
                tx = t_alt[li, 0, k, rows, :].astype(F32)
                ty = t_alt[li, 1, k, rows, :].astype(F32)
                txy = t_alt[li, 2, k, rows, :].astype(F32)
                inner = jnp.where(own_y, here, jnp.where(alt_y, ty, zero))
                outer = jnp.where(own_y, tx, jnp.where(alt_y, txy, zero))
                t_eff[li, slot, k, rows, :] = jnp.where(
                    own_x, inner, jnp.where(alt_x, outer, zero)
                ).astype(BF16)

    cl, sl = lane_ref[0, 0:1, :], lane_ref[1, 0:1, :]

    def right(z, first):
        head, tail = halves(z)
        table = jnp.concatenate([m_v[first], m_v[first], m_v[first + 1]], axis=0)
        return dot(jnp.concatenate([head, tail, head], axis=1), table)

    def left(z, first):
        head, tail = halves(z)
        table = jnp.concatenate([m_v[first], m_v[first + 1], m_v[first]], axis=1)
        return dot(table, jnp.concatenate([head, head, tail], axis=0))

    def right_forward(h, re, im):
        sr, dr = re[:, :HALF] + re[:, HALF:], re[:, :HALF] - re[:, HALF:]
        si, di = im[:, :HALF] + im[:, HALF:], im[:, :HALF] - im[:, HALF:]
        tr, ti = dr * cl + di * sl, di * cl - dr * sl
        z = jnp.concatenate(
            [jnp.concatenate([sr, si], axis=1), jnp.concatenate([tr, ti], axis=1)], axis=0
        )
        y = right(z, 2)
        zbuf[h, 0, :, :HALF] = y[:HALF, :HALF]
        zbuf[h, 0, :, HALF:] = y[HALF:, :HALF]
        zbuf[h, 1, :, :HALF] = y[:HALF, HALF:]
        zbuf[h, 1, :, HALF:] = y[HALF:, HALF:]

    def row_twiddle():
        c, s = rows_v[0], rows_v[1]
        return jnp.concatenate([c, c], axis=1), jnp.concatenate([s, s], axis=1)

    def spectrum():
        for h in (0, 1):
            if h == 0:
                zr, zi = zbuf[0, 0] + zbuf[1, 0], zbuf[0, 1] + zbuf[1, 1]
            else:
                c, s = row_twiddle()
                dr, di = zbuf[0, 0] - zbuf[1, 0], zbuf[0, 1] - zbuf[1, 1]
                zr, zi = dr * c + di * s, di * c - dr * s
            x = left(jnp.concatenate([zr, zi], axis=0), 0)
            xr, xi = x[:HALF], x[HALF:]
            cp, sp = rot[0, h], rot[1, h]
            y = jnp.concatenate([xr * cp + xi * sp, xi * cp - xr * sp], axis=0)
            e = left(y, 2)
            er, ei = e[:HALF], e[HALF:]
            if h == 1:
                er, ei = er * c - ei * s, ei * c + er * s
            ebuf[h, 0] = er
            ebuf[h, 1] = ei

    def right_inverse(h, store):
        if h == 0:
            vr, vi = ebuf[0, 0] + ebuf[1, 0], ebuf[0, 1] + ebuf[1, 1]
        else:
            vr, vi = ebuf[0, 0] - ebuf[1, 0], ebuf[0, 1] - ebuf[1, 1]
        z = jnp.concatenate(
            [
                jnp.concatenate([vr[:, :HALF], vi[:, :HALF]], axis=1),
                jnp.concatenate([vr[:, HALF:], vi[:, HALF:]], axis=1),
            ],
            axis=0,
        )
        y = right(z, 0)
        er, ei, orr, oi = y[:HALF, :HALF], y[:HALF, HALF:], y[HALF:, :HALF], y[HALF:, HALF:]
        tr, ti = orr * cl - oi * sl, oi * cl + orr * sl
        store(0, er + tr, er - tr)
        store(1, ei + ti, ei - ti)

    def through(li, slot, h, re, im):
        rows = part[h]
        tr = t_eff[li, slot, 0, rows, :].astype(F32)
        ti = t_eff[li, slot, 1, rows, :].astype(F32)
        right_forward(h, *conj_times(tr, ti, re, im))

    for li in (0, 1):
        g_own[li] = jnp.zeros((2, TILE, TILE), F32)
        for kind in range(3):
            g_alt[li, kind] = jnp.zeros((2, TILE, TILE), F32)

    def one_slot(slot, carry):
        @pl.when(slot == 0)
        def _():
            loads[5].wait()
            for c in t_copies(1):
                c.wait_recv()
            for s in (0, 1):
                window(1, s)

        for h in (0, 1):
            @pl.when(d < last)
            def _():
                w_copy(slot, h).wait_recv()

            through(1, slot, h, waves[slot, h, 0], waves[slot, h, 1])
        spectrum()
        for h in (0, 1):
            def keep(k, low, high, h=h):
                middle[slot, h, k, :, :HALF] = low
                middle[slot, h, k, :, HALF:] = high

            right_inverse(h, keep)

        @pl.when(slot == 0)
        def _():
            for c in t_copies(0):
                c.wait_recv()
            for s in (0, 1):
                window(0, s)

        @pl.when(d > 0)
        def _():
            for h in (0, 1):
                through(0, slot, h, middle[slot, h, 0], middle[slot, h, 1])
            spectrum()
            for h in (0, 1):
                def keep(k, low, high, h=h):
                    sent[slot, h, k, :, :HALF] = low
                    sent[slot, h, k, :, HALF:] = high

                right_inverse(h, keep)
                w_copy(slot, h).start()

        for li in (1, 0):
            wave = waves if li == 1 else middle
            for h in (0, 1):
                rows = part[h]
                own_x, own_y, alt_x, alt_y = masks(slot, h)
                er = inc[li, slot, 0, rows, :].astype(F32)
                ei = inc[li, slot, 1, rows, :].astype(F32)
                terms = conj_times(er, ei, wave[slot, h, 0], wave[slot, h, 1])
                for k, term in enumerate(terms):
                    g_own[li, k, rows, :] += jnp.where(own_x & own_y, term, zero)
                    g_alt[li, 0, k, rows, :] += jnp.where(alt_x & own_y, term, zero)
                    g_alt[li, 1, k, rows, :] += jnp.where(own_x & alt_y, term, zero)
                    g_alt[li, 2, k, rows, :] += jnp.where(alt_x & alt_y, term, zero)
        return carry

    lax.fori_loop(0, 2, one_slot, 0)

    for li in (1, 0):
        for c in g_copies(li):
            c.start()
    outs = []
    for li in (1, 0):
        for c in g_copies(li):
            c.wait_recv()
        for k in (0, 1):
            g_own[li, k] = (g_own[li, k] + g_in[li, 0, k]) + (g_in[li, 1, k] + g_in[li, 2, k])
        outs.append(pltpu.make_async_copy(g_own.at[li], out_hbm.at[li], out_sem.at[li]))
        outs[-1].start()

    for li in (1, 0):
        for c in t_copies(li):
            c.wait_send()
        for c in g_copies(li):
            c.wait_send()

    @pl.when(d > 0)
    def _():
        for slot in (0, 1):
            for h in (0, 1):
                w_copy(slot, h).wait_send()

    for c in outs:
        c.wait()


def shards(transmission, incident, exit_adjoint, propagator_phase, scan_anchor, live_count):
    sizes = tuple(lax.axis_size(a) for a in ("depth", "sx", "sy"))
    slab = transmission.shape[0]
    rows, lanes = twiddles()
    any_space = pl.BlockSpec(memory_space=pl.ANY)
    smem = pl.BlockSpec(memory_space=pltpu.SMEM)
    plane = (TILE, TILE)
    dma = pltpu.SemaphoreType.DMA
    return pl.pallas_call(
        functools.partial(kernel, sizes),
        out_shape=jax.ShapeDtypeStruct(transmission.shape, F32),
        in_specs=[any_space] * 6 + [pl.BlockSpec(memory_space=pltpu.VMEM), smem, smem],
        out_specs=any_space,
        scratch_shapes=[
            pltpu.VMEM((slab, 2) + plane, BF16),
            pltpu.VMEM((slab, 3, 2) + plane, BF16),
            pltpu.VMEM((slab, 2, 2) + plane, BF16),
            pltpu.VMEM((slab, 2, 2) + plane, BF16),
            pltpu.VMEM((2, 2) + plane, BF16),
            pltpu.VMEM(plane, F32),
            pltpu.VMEM((2, 2, HALF, TILE), F32),
            pltpu.VMEM((4,) + plane, BF16),
            pltpu.VMEM((2, HALF, HALF), F32),
            pltpu.VMEM((2, 2, 2, HALF, TILE), F32),
            pltpu.VMEM((2, 2, 2, HALF, TILE), F32),
            pltpu.VMEM((2, 2, 2, HALF, TILE), F32),
            pltpu.VMEM((2, 2, HALF, TILE), F32),
            pltpu.VMEM((2, 2, HALF, TILE), F32),
            pltpu.VMEM((slab, 2) + plane, F32),
            pltpu.VMEM((slab, 3, 2) + plane, F32),
            pltpu.VMEM((slab, 3, 2) + plane, F32),
            dma((6,)),
            dma((16,)),
            dma((16,)),
            dma((4,)),
            dma((4,)),
            dma((16,)),
            dma((16,)),
            dma((2,)),
        ],
        compiler_params=pltpu.CompilerParams(
            collective_id=0, has_side_effects=True, vmem_limit_bytes=60 * 1024 * 1024
        ),
    )(
        transmission,
        incident,
        exit_adjoint,
        propagator_phase,
        jnp.asarray(dft_tables()),
        jnp.asarray(rows),
        jnp.asarray(lanes),
        scan_anchor,
        live_count,
    )


def solution(mesh):
    placed = (
        P("depth", None, "sx", "sy"),
        P("depth", ("sx", "sy"), None, None, None),
        P(("sx", "sy"), None, None, None),
        P(),
        P(("sx", "sy"), None),
        P(("sx", "sy")),
    )
    return jax.shard_map(
        shards, mesh=mesh, in_specs=placed, out_specs=P("depth", None, "sx", "sy"), check_vma=False
    )
```

profile of v0, /device:TPU:8, one launch (start us, length us, event | category | flops | bytes accessed | tf_op | source)
XLA Modules:
  0.0 116.1 jit_solution(13974036073813445705)
XLA Ops:
  0.7 113.1 %shard_map.91 = f32[2,2,256,256]{3,2,1,0:T(8,128)} custom-call(bf16[2,2,256,256]{3,2,1,0:T(8,128)(2,1)} %t_hbm.1, bf16[2,2,2,256,256]{4,3,2,1,0:T(8,128)(2,1)} %inc_hbm.1, bf16[2,2,256,256]{3,2,1,0:T(8,128)(2,1)} %exit_hbm.1, f32[256,256]{1,0:T(8,128)} %phase_hbm.1, bf16[4,256,256]{2,1,0:T(8,128)(2,1)} %constant.6.clone.m_hbm, ...), custom_call_target="tpu_custom_call" | custom-call | tf_op jit(solution)/shard_map/pallas_call | solution.py:426
  113.8 2.3 %copy.12 = f32[2,2,256,256]{3,2,1,0:T(8,128)} copy(f32[2,2,256,256]{3,2,1,0:T(8,128)} %shard_map.91) | data formatting | bytes 2097152
where the time goes:
time: 116 us
  Pallas kernels  113 us (97%)
  local copies, waits for them, and re-layouts  2.29 us (2%)
    pallas_call x1, Pallas kernels, shards(): pl.pallas_call(functools.partial(kernel, sizes), out_shape=jax.ShapeDtype...  113 us

commit v1 on v0

--- a/solution.py
+++ b/solution.py
@@ -11,6 +11,8 @@
 
 TILE = 256
 HALF = 128
+GROUPS = HALF // 8
+CODED = HALF + 8
 MESH = pl.DeviceIdType.MESH
 F32 = jnp.float32
 BF16 = jnp.bfloat16
@@ -44,6 +46,30 @@
 
 def conj_times(ar, ai, br, bi):
     return ar * br + ai * bi, ar * bi - ai * br
+
+
+def spread(x):
+    return jnp.concatenate([x] * GROUPS, axis=0)
+
+
+def coded(re, im):
+    top = jnp.maximum(jnp.abs(re), jnp.abs(im))
+    parts = [top[8 * g : 8 * g + 8] for g in range(GROUPS)]
+    while len(parts) > 1:
+        parts = [jnp.maximum(a, b) for a, b in zip(parts[::2], parts[1::2])]
+    steps = (jnp.log2(jnp.maximum(parts[0], 1e-33)) * 8.0).astype(jnp.int32) + 2
+    unit = spread(32767.0 / jnp.exp2(steps.astype(F32) * 0.125))
+    high = (re * unit + 32768.5).astype(jnp.int32)
+    low = (im * unit + 32768.5).astype(jnp.int32)
+    return jnp.concatenate([(high << 16) | low, steps], axis=0)
+
+
+def decoded(words):
+    unit = spread(jnp.exp2(words[HALF:].astype(F32) * 0.125) * (1.0 / 32767.0))
+    body = words[:HALF]
+    high = ((body >> 16) & 65535).astype(F32) - 32768.0
+    low = (body & 65535).astype(F32) - 32768.0
+    return high * unit, low * unit
 
 
 def dot(a, b):
@@ -73,11 +99,13 @@
     rows_v,
     waves,
     middle,
-    sent,
+    words_in,
+    words_out,
     zbuf,
     ebuf,
     g_own,
     g_alt,
+    g_out,
     g_in,
     load_sem,
     t_send,
@@ -87,6 +115,7 @@
     g_send,
     g_recv,
     out_sem,
+    go,
 ):
     n_depth, n_sx, n_sy = sizes
     d, sx, sy = lax.axis_index("depth"), lax.axis_index("sx"), lax.axis_index("sy")
@@ -131,6 +160,14 @@
         + [(2, part[p], part[q], (toward[p], toward[q])) for p in (0, 1) for q in (0, 1)]
     )
 
+    both = pl.ds(0, 2)
+    one = [pl.ds(0, 1), pl.ds(1, 1)]
+    blocks = (
+        [(0, (one[p], both), (toward[p], 0)) for p in (0, 1)]
+        + [(1, (both, one[q]), (0, toward[q])) for q in (0, 1)]
+        + [(2, (one[p], one[q]), (toward[p], toward[q])) for p in (0, 1) for q in (0, 1)]
+    )
+
     def t_copies(li):
         return [
             pltpu.make_async_remote_copy(
@@ -147,29 +184,36 @@
     def g_copies(li):
         return [
             pltpu.make_async_remote_copy(
-                src_ref=g_alt.at[li, kind, :, rows, lanes],
-                dst_ref=g_in.at[li, kind, :, rows, lanes],
+                src_ref=g_out.at[li, kind, block[0], block[1]],
+                dst_ref=g_in.at[li, kind, block[0], block[1]],
                 send_sem=g_send.at[li * 8 + i],
                 recv_sem=g_recv.at[li * 8 + i],
                 device_id=at(-way[0], -way[1]),
                 device_id_type=MESH,
             )
-            for i, (kind, rows, lanes, way) in enumerate(pieces)
+            for i, (kind, block, way) in enumerate(blocks)
         ]
 
     def w_copy(slot, h):
         return pltpu.make_async_remote_copy(
-            src_ref=sent.at[slot, h],
-            dst_ref=waves.at[slot, h],
+            src_ref=words_out.at[slot, h],
+            dst_ref=words_in.at[slot, h],
             send_sem=w_send.at[slot * 2 + h],
             recv_sem=w_recv.at[slot * 2 + h],
             device_id=(lax.rem(d + last, n_depth), sx, sy),
             device_id_type=MESH,
         )
 
-    for li in (1, 0):
-        for c in t_copies(li):
-            c.start()
+    odd = lax.rem(d, 2) == 1
+
+    def share():
+        for li in (1, 0):
+            for c in t_copies(li):
+                c.start()
+
+    @pl.when(odd)
+    def _():
+        share()
 
     def offsets(slot):
         return anchor_ref[slot, 0] - sx * TILE, anchor_ref[slot, 1] - sy * TILE
@@ -313,8 +357,7 @@
         y = right(z, 0)
         er, ei, orr, oi = y[:HALF, :HALF], y[:HALF, HALF:], y[HALF:, :HALF], y[HALF:, HALF:]
         tr, ti = orr * cl - oi * sl, oi * cl + orr * sl
-        store(0, er + tr, er - tr)
-        store(1, ei + ti, ei - ti)
+        store(er + tr, er - tr, ei + ti, ei - ti)
 
     def through(li, slot, h, re, im):
         rows = part[h]
@@ -327,28 +370,83 @@
         for kind in range(3):
             g_alt[li, kind] = jnp.zeros((2, TILE, TILE), F32)
 
-    def one_slot(slot, carry):
-        @pl.when(slot == 0)
-        def _():
-            loads[5].wait()
-            for c in t_copies(1):
-                c.wait_recv()
-            for s in (0, 1):
-                window(1, s)
-
+    def gradient(li, slot):
+        wave = waves if li == 1 else middle
         for h in (0, 1):
-            @pl.when(d < last)
-            def _():
-                w_copy(slot, h).wait_recv()
-
-            through(1, slot, h, waves[slot, h, 0], waves[slot, h, 1])
+            rows = part[h]
+            own_x, own_y, alt_x, alt_y = masks(slot, h)
+            er = inc[li, slot, 0, rows, :].astype(F32)
+            ei = inc[li, slot, 1, rows, :].astype(F32)
+            terms = conj_times(er, ei, wave[slot, h, 0], wave[slot, h, 1])
+            for k, term in enumerate(terms):
+                g_own[li, k, rows, :] += jnp.where(own_x & own_y, term, zero)
+                g_alt[li, 0, k, rows, :] += jnp.where(alt_x & own_y, term, zero)
+                g_alt[li, 1, k, rows, :] += jnp.where(own_x & alt_y, term, zero)
+                g_alt[li, 2, k, rows, :] += jnp.where(alt_x & alt_y, term, zero)
+
+    def hand_over(li):
+        for kind in (2, 0, 1):
+            for p in (0, 1):
+                for q in (0, 1):
+                    g_out[li, kind, p, q] = coded(
+                        g_alt[li, kind, 0, part[p], part[q]], g_alt[li, kind, 1, part[p], part[q]]
+                    )
+        for c in g_copies(li):
+            c.start()
+
+    def apply_layer(li, slot, source, store, done):
+        for h in (0, 1):
+            through(li, slot, h, source[slot, h, 0], source[slot, h, 1])
         spectrum()
         for h in (0, 1):
-            def keep(k, low, high, h=h):
-                middle[slot, h, k, :, :HALF] = low
-                middle[slot, h, k, :, HALF:] = high
-
-            right_inverse(h, keep)
+            right_inverse(h, functools.partial(store, h))
+            done(h)
+
+    loads[5].wait()
+
+    @pl.when(odd)
+    def _():
+        for c in t_copies(1):
+            c.wait_recv()
+        pl.semaphore_signal(go, inc=1, device_id=(d - 1, sx, sy), device_id_type=MESH)
+
+    @pl.when(jnp.logical_not(odd))
+    def _():
+        pl.semaphore_wait(go, 1)
+        share()
+        for c in t_copies(1):
+            c.wait_recv()
+
+    for slot in (0, 1):
+        window(1, slot)
+
+    early = d < 2
+
+    def one_slot(slot, carry):
+        @pl.when(d < last)
+        def _():
+            for h in (0, 1):
+                w_copy(slot, h).wait_recv()
+                for q in (0, 1):
+                    re, im = decoded(words_in[slot, h, q])
+                    waves[slot, h, 0, :, part[q]] = re
+                    waves[slot, h, 1, :, part[q]] = im
+
+        @pl.when(early)
+        def _():
+            gradient(1, slot)
+
+            @pl.when(slot == 1)
+            def _():
+                hand_over(1)
+
+        def keep(h, lr, hr, li_, hi_):
+            middle[slot, h, 0, :, :HALF] = lr
+            middle[slot, h, 0, :, HALF:] = hr
+            middle[slot, h, 1, :, :HALF] = li_
+            middle[slot, h, 1, :, HALF:] = hi_
+
+        apply_layer(1, slot, waves, keep, lambda h: None)
 
         @pl.when(slot == 0)
         def _():
@@ -357,45 +455,46 @@
             for s in (0, 1):
                 window(0, s)
 
+        @pl.when(early)
+        def _():
+            gradient(0, slot)
+
+            @pl.when(slot == 1)
+            def _():
+                hand_over(0)
+
         @pl.when(d > 0)
         def _():
-            for h in (0, 1):
-                through(0, slot, h, middle[slot, h, 0], middle[slot, h, 1])
-            spectrum()
-            for h in (0, 1):
-                def keep(k, low, high, h=h):
-                    sent[slot, h, k, :, :HALF] = low
-                    sent[slot, h, k, :, HALF:] = high
-
-                right_inverse(h, keep)
-                w_copy(slot, h).start()
-
+            def encode(h, lr, hr, li_, hi_):
+                words_out[slot, h, 0] = coded(lr, li_)
+                words_out[slot, h, 1] = coded(hr, hi_)
+
+            apply_layer(0, slot, middle, encode, lambda h: w_copy(slot, h).start())
+
+        return carry
+
+    lax.fori_loop(0, 2, one_slot, 0)
+
+    @pl.when(jnp.logical_not(early))
+    def _():
         for li in (1, 0):
-            wave = waves if li == 1 else middle
-            for h in (0, 1):
-                rows = part[h]
-                own_x, own_y, alt_x, alt_y = masks(slot, h)
-                er = inc[li, slot, 0, rows, :].astype(F32)
-                ei = inc[li, slot, 1, rows, :].astype(F32)
-                terms = conj_times(er, ei, wave[slot, h, 0], wave[slot, h, 1])
-                for k, term in enumerate(terms):
-                    g_own[li, k, rows, :] += jnp.where(own_x & own_y, term, zero)
-                    g_alt[li, 0, k, rows, :] += jnp.where(alt_x & own_y, term, zero)
-                    g_alt[li, 1, k, rows, :] += jnp.where(own_x & alt_y, term, zero)
-                    g_alt[li, 2, k, rows, :] += jnp.where(alt_x & alt_y, term, zero)
-        return carry
-
-    lax.fori_loop(0, 2, one_slot, 0)
-
-    for li in (1, 0):
-        for c in g_copies(li):
-            c.start()
+            def both_slots(slot, carry, li=li):
+                gradient(li, slot)
+                return carry
+
+            lax.fori_loop(0, 2, both_slots, 0)
+            hand_over(li)
+
     outs = []
     for li in (1, 0):
         for c in g_copies(li):
             c.wait_recv()
-        for k in (0, 1):
-            g_own[li, k] = (g_own[li, k] + g_in[li, 0, k]) + (g_in[li, 1, k] + g_in[li, 2, k])
+        for p in (0, 1):
+            for q in (0, 1):
+                got = [decoded(g_in[li, kind, p, q]) for kind in range(3)]
+                for k in (0, 1):
+                    total = (got[0][k] + got[1][k]) + got[2][k]
+                    g_own[li, k, part[p], part[q]] += total
         outs.append(pltpu.make_async_copy(g_own.at[li], out_hbm.at[li], out_sem.at[li]))
         outs[-1].start()
 
@@ -440,12 +539,14 @@
             pltpu.VMEM((2, HALF, HALF), F32),
             pltpu.VMEM((2, 2, 2, HALF, TILE), F32),
             pltpu.VMEM((2, 2, 2, HALF, TILE), F32),
-            pltpu.VMEM((2, 2, 2, HALF, TILE), F32),
+            pltpu.VMEM((2, 2, 2, CODED, HALF), jnp.int32),
+            pltpu.VMEM((2, 2, 2, CODED, HALF), jnp.int32),
             pltpu.VMEM((2, 2, HALF, TILE), F32),
             pltpu.VMEM((2, 2, HALF, TILE), F32),
             pltpu.VMEM((slab, 2) + plane, F32),
             pltpu.VMEM((slab, 3, 2) + plane, F32),
-            pltpu.VMEM((slab, 3, 2) + plane, F32),
+            pltpu.VMEM((slab, 3, 2, 2, CODED, HALF), jnp.int32),
+            pltpu.VMEM((slab, 3, 2, 2, CODED, HALF), jnp.int32),
             dma((6,)),
             dma((16,)),
             dma((16,)),
@@ -454,6 +555,7 @@
             dma((16,)),
             dma((16,)),
             dma((2,)),
+            pltpu.SemaphoreType.REGULAR,
         ],
         compiler_params=pltpu.CompilerParams(
             collective_id=0, has_side_effects=True, vmem_limit_bytes=60 * 1024 * 1024

time: 116 us -> 91.8 us (0.79)
  Pallas kernels: 113 us -> 88.6 us
    pallas_call x1, Pallas kernels: 113 us -> 88.6 us  [shards(): pl.pallas_call(functools.partial(kernel, sizes), out_shape=jax.ShapeDtype...]
where the time goes in v1:
time: 91.8 us; the launch traced here: 91.6 us
  Pallas kernels  88.6 us (97%)
  local copies, waits for them, and re-layouts  2.29 us (2%)
    pallas_call x1, Pallas kernels, shards(): pl.pallas_call(functools.partial(kernel, sizes), out_shape=jax.ShapeDtype...  88.6 us
    unnamed x1, local copies, waits for them, and re-layouts  2.29 us

profile of v1, /device:TPU:8, one launch (start us, length us, event | category | flops | bytes accessed | tf_op | source)
XLA Modules:
  0.0 91.6 jit_solution(1532391102001484396)
XLA Ops:
  0.7 88.6 %shard_map.91 = f32[2,2,256,256]{3,2,1,0:T(8,128)} custom-call(bf16[2,2,256,256]{3,2,1,0:T(8,128)(2,1)} %t_hbm.1, bf16[2,2,2,256,256]{4,3,2,1,0:T(8,128)(2,1)} %inc_hbm.1, bf16[2,2,256,256]{3,2,1,0:T(8,128)(2,1)} %exit_hbm.1, f32[256,256]{1,0:T(8,128)} %phase_hbm.1, bf16[4,256,256]{2,1,0:T(8,128)(2,1)} %constant.6.clone.m_hbm, ...), custom_call_target="tpu_custom_call" | custom-call | tf_op jit(solution)/shard_map/pallas_call | solution.py:525
  89.3 2.3 %copy.12 = f32[2,2,256,256]{3,2,1,0:T(8,128)} copy(f32[2,2,256,256]{3,2,1,0:T(8,128)} %shard_map.91) | data formatting | bytes 2097152
